TPU v7x, 32 devices: a whole 2x2x4 slice. The times are simulated.
32 devices in a mesh: sec: 4 (over x, core), row: 4 (over z), col: 2 (over y).
Axes of the slice: x: 2, y: 2, z: 4, core: 2. Of those that a mesh axis runs over, the one named last changes fastest.
Arguments:
- forcing: float32 [4, 8192, 128], P('sec', ('row', 'col')), may hold values from -6 to 6
- inverse_factor: bfloat16 [4, 2, 8192, 8192], P('sec', None, 'col', 'row'), as said below
- diag_inverse: float32 [4, 2, 8192], P('sec', None, 'col'), may hold values from -0.6 to 0.6
- coupling: float32 [4, 2, 8192], P('sec', None, ('row', 'col')), may hold values from -0.8 to 0.8
Outputs:
- section_fields: float32 [4, 8192, 128], P('sec', ('row', 'col'))
Inputs may be any that keep to these rules, and one draw needn't show every extreme that they name: `inverse_factor`: each section's factor is lower triangular: entries above the diagonal are zero in both parts.
All inputs are finite; a program needn't handle non-finite values.
Results may differ from a plain program's by a relative error of at most 0.03.
Values may be sent and summed in bfloat16 or wider, within the bound.
A program may use at most 128 MiB of HBM per device.

v0:
```python
import jax
import jax.numpy as jnp
from jax import lax
from jax.sharding import PartitionSpec as P


def shifted(value, axis, steps):
    count = lax.axis_size(axis)
    initial, last = (max(0, -steps), min(count, count - steps))
    return lax.ppermute(value, axis, [(source, source + steps) for source in range(initial, last)])


def complex_rows(coef_re, coef_im, values, half):
    v_re = values[:, :half]
    v_im = values[:, half:]
    out_re = coef_re[:, None] * v_re - coef_im[:, None] * v_im
    out_im = coef_re[:, None] * v_im + coef_im[:, None] * v_re
    return jnp.concatenate([out_re, out_im], axis=1)


def combine_stack(product):
    half = product.shape[2] // 2
    out_re = product[0, :, :half] - product[1, :, half:]
    out_im = product[0, :, half:] + product[1, :, :half]
    return jnp.concatenate([out_re, out_im], axis=1)


def solve_section(source, factor, dinv):
    width = source.shape[1]
    product = jnp.einsum(
        "kij,jb->kib",
        factor,
        lax.all_gather(source, "col", axis=0, tiled=True),
        preferred_element_type=jnp.float32,
    )
    forward = combine_stack(product)
    share = lax.psum_scatter(
        forward.astype(jnp.bfloat16), "row", scatter_dimension=0, tiled=True
    ).astype(jnp.float32)
    share_rows = share.shape[0]
    local_dinv = lax.dynamic_slice_in_dim(dinv, lax.axis_index("row") * share_rows, share_rows, 1)
    scaled = complex_rows(local_dinv[0], local_dinv[1], share, width // 2).astype(jnp.bfloat16)
    product = jnp.einsum(
        "kij,ib->kjb",
        factor,
        lax.all_gather(scaled, "row", axis=0, tiled=True),
        preferred_element_type=jnp.float32,
    )
    back = combine_stack(product)
    return lax.psum_scatter(
        back.astype(jnp.bfloat16), "col", scatter_dimension=0, tiled=True
    ).astype(jnp.float32)


def local(forcing, inverse_factor, diag_inverse, coupling):
    sections = lax.axis_size("sec")
    section_id = lax.axis_index("sec")
    local_rhs = forcing[0]
    factor = inverse_factor[0]
    dinv = diag_inverse[0]
    couple = coupling[0]
    rows_here = local_rhs.shape[0]
    half = local_rhs.shape[1] // 2
    block_count = 1
    block_width = half // block_count
    rhs_blocks = local_rhs.reshape(rows_here, 2, block_count, block_width)
    results = jnp.zeros((rows_here, 2, block_count, block_width), jnp.float32)
    outgoing = jnp.zeros((rows_here, 2 * block_width), jnp.float32)
    for step_index in range(block_count + sections - 1):
        if step_index > 0:
            incoming = shifted(outgoing.astype(jnp.bfloat16), "sec", 1).astype(outgoing.dtype)
        else:
            incoming = jnp.zeros((rows_here, 2 * block_width), jnp.float32)
        block_index = step_index - section_id
        active = jnp.logical_and(block_index >= 0, block_index < block_count)
        safe_index = jnp.clip(block_index, 0, block_count - 1)
        current = lax.dynamic_index_in_dim(rhs_blocks, safe_index, 2, keepdims=False)
        current = current.reshape(rows_here, 2 * block_width)
        source = (current - complex_rows(couple[0], couple[1], incoming, block_width)).astype(
            jnp.bfloat16
        )
        field = solve_section(source, factor, dinv)
        updated = lax.dynamic_update_index_in_dim(
            results, field.reshape(rows_here, 2, block_width), safe_index, 2
        )
        results = jnp.where(active, updated, results)
        outgoing = field
    return results.reshape(1, rows_here, 2 * half)


def solution(mesh):
    placed = (
        P("sec", ("row", "col"), None),
        P("sec", None, "col", "row"),
        P("sec", None, "col"),
        P("sec", None, ("row", "col")),
    )
    return jax.shard_map(
        local, mesh=mesh, in_specs=placed, out_specs=P("sec", ("row", "col"), None), check_vma=False
    )
```

profile of v0, /device:TPU:0, one launch (start us, length us, event | category | flops | bytes accessed | tf_op | source)
XLA Modules:
  0.0 482.2 jit_solution(10238314074252563666)
XLA Ops:
  6.5 0.8 fusion.84
  7.3 1.2 copy.5
  8.7 9.9 %all_gather.24 = bf16[2048,128]{0,1:T(8,128)(2,1)S(1)} all-gather(bf16[1024,128]{0,1:T(8,128)(2,1)S(1)} %fusion.68), channel_id=1, replica_groups=mesh['sec'=4,'row'=4,'col'=2] {'col'}, dimensions={0}, use_global_device_ids=true | all-gather | bytes 786432 | tf_op jit(solution)/shard_map/all_gather | solution.py:33
  18.6 16.3 %fusion.16 = f32[2,4096,128]{1,2,0:T(8,128)S(1)} fusion(bf16[1,2,4096,2048]{3,2,1,0:T(8,128)(2,1)} %param.5, bf16[2048,128]{0,1:T(8,128)(2,1)S(1)} %all_gather.24), kind=kOutput, calls=%fused_computation.16 | convolution fusion | flops 4294967296 | bytes 38273024 | tf_op jit(solution)/shard_map/kij,jb->kib/dot_general | solution.py:30
  35.2 1.1 pad_maximum_fusion
  36.3 0.9 constant_dynamic-slice_fusion
  37.2 27.9 %reduce-scatter.9.cloned.1.call-done = bf16[1024,128]{0,1:T(8,128)(2,1)} async-done(((bf16[4096,128]{0,1:T(8,128)(2,1)}), bf16[1024,128]{0,1:T(8,128)(2,1)}) %reduce-scatter.9.cloned.1.call-update) | async-done | bytes 262160 | tf_op jit(solution)/shard_map/reduce_scatter | solution.py:37
  65.1 1.0 convert_element_type.61
  66.1 0.7 pad_maximum_fusion.8
  66.9 26.7 %all-gather.5.cloned.1.call-done = bf16[4096,128]{0,1:T(8,128)(2,1)} async-done(((bf16[1024,128]{0,1:T(8,128)(2,1)}), bf16[4096,128]{0,1:T(8,128)(2,1)}) %all-gather.5.cloned.1.call-update) | async-done | bytes 1048592 | tf_op jit(solution)/shard_map/all_gather | solution.py:46
  93.6 13.2 %fusion.28 = f32[2,2048,128]{1,2,0:T(8,128)S(1)} fusion(bf16[1,2,4096,2048]{3,2,1,0:T(8,128)(2,1)} %param.5, bf16[4096,128]{0,1:T(8,128)(2,1)} %all-gather.5.cloned.1.call-done), kind=kOutput, calls=%fused_computation.20 | convolution fusion | flops 4294967296 | bytes 36700160 | tf_op jit(solution)/shard_map/kij,ib->kjb/dot_general | solution.py:43
  107.0 0.8 pad_maximum_fusion.4
  107.9 14.2 %reduce-scatter.11.cloned.1.call-done = bf16[1024,128]{0,1:T(8,128)(2,1)} async-done(((bf16[2048,128]{0,1:T(8,128)(2,1)}), bf16[1024,128]{0,1:T(8,128)(2,1)}) %reduce-scatter.11.cloned.1.call-update) | async-done | bytes 262160 | tf_op jit(solution)/shard_map/reduce_scatter | solution.py:50
  122.0 1.7 collective-permute-start
  123.8 1.3 collective-permute-done
  125.3 7.0 %all_gather.26 = bf16[2048,128]{0,1:T(8,128)(2,1)S(1)} all-gather(bf16[1024,128]{0,1:T(8,128)(2,1)S(1)} %fusion.69), channel_id=1, replica_groups=mesh['sec'=4,'row'=4,'col'=2] {'col'}, dimensions={0}, use_global_device_ids=true | all-gather | bytes 786432 | tf_op jit(solution)/shard_map/all_gather | solution.py:33
  132.4 16.3 %fusion.19 = f32[2,4096,128]{1,2,0:T(8,128)S(1)} fusion(bf16[1,2,4096,2048]{3,2,1,0:T(8,128)(2,1)} %param.5, bf16[2048,128]{0,1:T(8,128)(2,1)S(1)} %all_gather.26), kind=kOutput, calls=%fused_computation.17 | convolution fusion | flops 4294967296 | bytes 38273024 | tf_op jit(solution)/shard_map/kij,jb->kib/dot_general | solution.py:30
  148.9 1.1 pad_maximum_fusion.1
  150.0 32.0 %reduce-scatter.13.cloned.1.call-done = bf16[1024,128]{0,1:T(8,128)(2,1)} async-done(((bf16[4096,128]{0,1:T(8,128)(2,1)}), bf16[1024,128]{0,1:T(8,128)(2,1)}) %reduce-scatter.13.cloned.1.call-update) | async-done | bytes 262160 | tf_op jit(solution)/shard_map/reduce_scatter | solution.py:37
  182.1 1.0 convert_element_type.64
  184.1 26.5 %all-gather.7.cloned.1.call-done = bf16[4096,128]{0,1:T(8,128)(2,1)} async-done(((bf16[1024,128]{0,1:T(8,128)(2,1)}), bf16[4096,128]{0,1:T(8,128)(2,1)}) %all-gather.7.cloned.1.call-update) | async-done | bytes 1048592 | tf_op jit(solution)/shard_map/all_gather | solution.py:46
  210.6 13.2 %fusion.31 = f32[2,2048,128]{1,2,0:T(8,128)S(1)} fusion(bf16[1,2,4096,2048]{3,2,1,0:T(8,128)(2,1)} %param.5, bf16[4096,128]{0,1:T(8,128)(2,1)} %all-gather.7.cloned.1.call-done), kind=kOutput, calls=%fused_computation.21 | convolution fusion | flops 4294967296 | bytes 36700160 | tf_op jit(solution)/shard_map/kij,ib->kjb/dot_general | solution.py:43
  224.0 0.8 pad_maximum_fusion.5
  224.9 14.2 %reduce-scatter.15.cloned.1.call-done = bf16[1024,128]{0,1:T(8,128)(2,1)} async-done(((bf16[2048,128]{0,1:T(8,128)(2,1)}), bf16[1024,128]{0,1:T(8,128)(2,1)}) %reduce-scatter.15.cloned.1.call-update) | async-done | bytes 262160 | tf_op jit(solution)/shard_map/reduce_scatter | solution.py:50
  239.0 1.7 collective-permute-start.1
  240.8 1.3 collective-permute-done.1
  242.3 7.0 %all_gather.28 = bf16[2048,128]{0,1:T(8,128)(2,1)S(1)} all-gather(bf16[1024,128]{0,1:T(8,128)(2,1)S(1)} %fusion.70), channel_id=1, replica_groups=mesh['sec'=4,'row'=4,'col'=2] {'col'}, dimensions={0}, use_global_device_ids=true | all-gather | bytes 786432 | tf_op jit(solution)/shard_map/all_gather | solution.py:33
  249.3 16.3 %fusion.22 = f32[2,4096,128]{1,2,0:T(8,128)S(1)} fusion(bf16[1,2,4096,2048]{3,2,1,0:T(8,128)(2,1)} %param.5, bf16[2048,128]{0,1:T(8,128)(2,1)S(1)} %all_gather.28), kind=kOutput, calls=%fused_computation.18 | convolution fusion | flops 4294967296 | bytes 38273024 | tf_op jit(solution)/shard_map/kij,jb->kib/dot_general | solution.py:30
  265.9 1.1 pad_maximum_fusion.2
  267.0 32.0 %reduce-scatter.17.cloned.1.call-done = bf16[1024,128]{0,1:T(8,128)(2,1)} async-done(((bf16[4096,128]{0,1:T(8,128)(2,1)}), bf16[1024,128]{0,1:T(8,128)(2,1)}) %reduce-scatter.17.cloned.1.call-update) | async-done | bytes 262160 | tf_op jit(solution)/shard_map/reduce_scatter | solution.py:37
  299.0 1.0 convert_element_type.67
  300.9 26.7 %all-gather.9.cloned.1.call-done = bf16[4096,128]{0,1:T(8,128)(2,1)} async-done(((bf16[1024,128]{0,1:T(8,128)(2,1)}), bf16[4096,128]{0,1:T(8,128)(2,1)}) %all-gather.9.cloned.1.call-update) | async-done | bytes 1048592 | tf_op jit(solution)/shard_map/all_gather | solution.py:46
  327.6 13.2 %fusion.34 = f32[2,2048,128]{1,2,0:T(8,128)S(1)} fusion(bf16[1,2,4096,2048]{3,2,1,0:T(8,128)(2,1)} %param.5, bf16[4096,128]{0,1:T(8,128)(2,1)} %all-gather.9.cloned.1.call-done), kind=kOutput, calls=%fused_computation.22 | convolution fusion | flops 4294967296 | bytes 36700160 | tf_op jit(solution)/shard_map/kij,ib->kjb/dot_general | solution.py:43
  340.9 0.8 pad_maximum_fusion.6
  341.8 14.2 %reduce-scatter.19.cloned.1.call-done = bf16[1024,128]{0,1:T(8,128)(2,1)} async-done(((bf16[2048,128]{0,1:T(8,128)(2,1)}), bf16[1024,128]{0,1:T(8,128)(2,1)}) %reduce-scatter.19.cloned.1.call-update) | async-done | bytes 262160 | tf_op jit(solution)/shard_map/reduce_scatter | solution.py:50
  356.0 1.7 collective-permute-start.2
  357.7 1.3 collective-permute-done.2
  359.2 7.3 %all_gather.30 = bf16[2048,128]{0,1:T(8,128)(2,1)S(1)} all-gather(bf16[1024,128]{0,1:T(8,128)(2,1)S(1)} %fusion.71), channel_id=1, replica_groups=mesh['sec'=4,'row'=4,'col'=2] {'col'}, dimensions={0}, use_global_device_ids=true | all-gather | bytes 786432 | tf_op jit(solution)/shard_map/all_gather | solution.py:33
  366.5 16.3 %fusion.25 = f32[2,4096,128]{1,2,0:T(8,128)S(1)} fusion(bf16[1,2,4096,2048]{3,2,1,0:T(8,128)(2,1)} %param.5, bf16[2048,128]{0,1:T(8,128)(2,1)S(1)} %all_gather.30), kind=kOutput, calls=%fused_computation.19 | convolution fusion | flops 4294967296 | bytes 38273024 | tf_op jit(solution)/shard_map/kij,jb->kib/dot_general | solution.py:30
  383.0 1.1 pad_maximum_fusion.3
  384.2 32.0 %reduce-scatter.21.cloned.1.call-done = bf16[1024,128]{0,1:T(8,128)(2,1)} async-done(((bf16[4096,128]{0,1:T(8,128)(2,1)}), bf16[1024,128]{0,1:T(8,128)(2,1)}) %reduce-scatter.21.cloned.1.call-update) | async-done | bytes 262160 | tf_op jit(solution)/shard_map/reduce_scatter | solution.py:37
  416.2 1.0 convert_element_type.70
  418.1 26.7 %all-gather.11.cloned.1.call-done = bf16[4096,128]{0,1:T(8,128)(2,1)} async-done(((bf16[1024,128]{0,1:T(8,128)(2,1)}), bf16[4096,128]{0,1:T(8,128)(2,1)}) %all-gather.11.cloned.1.call-update) | async-done | bytes 1048592 | tf_op jit(solution)/shard_map/all_gather | solution.py:46
  444.8 13.2 %fusion.37 = f32[2,2048,128]{1,2,0:T(8,128)S(1)} fusion(bf16[1,2,4096,2048]{3,2,1,0:T(8,128)(2,1)} %param.5, bf16[4096,128]{0,1:T(8,128)(2,1)} %all-gather.11.cloned.1.call-done), kind=kOutput, calls=%fused_computation.23 | convolution fusion | flops 4294967296 | bytes 36700160 | tf_op jit(solution)/shard_map/kij,ib->kjb/dot_general | solution.py:43
  458.1 0.8 pad_maximum_fusion.7
  459.0 14.2 %reduce-scatter.23.cloned.1.call-done = bf16[1024,128]{0,1:T(8,128)(2,1)} async-done(((bf16[2048,128]{0,1:T(8,128)(2,1)}), bf16[1024,128]{0,1:T(8,128)(2,1)}) %reduce-scatter.23.cloned.1.call-update) | async-done | bytes 262160 | tf_op jit(solution)/shard_map/reduce_scatter | solution.py:50
  473.2 1.1 select_bitcast_fusion
  474.3 1.0 copy.6
  (58 shorter events, 5.2 us)
Async XLA Ops:
  6.5 58.5 %reduce-scatter.9.cloned.1.call-start = ((), (), s32[]{:S(2)}) async-start(), calls=%async_computation.8 | async-start | bytes 1310720 | tf_op jit(solution)/shard_map/reduce_scatter | solution.py:37
  36.3 57.4 %all-gather.5.cloned.1.call-start = ((), (), s32[]{:S(2)}) async-start(), calls=%async_computation.9 | async-start | bytes 1310720 | tf_op jit(solution)/shard_map/all_gather | solution.py:46
  66.9 55.1 %reduce-scatter.11.cloned.1.call-start = ((), (), s32[]{:S(2)}) async-start(), calls=%async_computation.10 | async-start | bytes 786432 | tf_op jit(solution)/shard_map/reduce_scatter | solution.py:50
  107.8 74.2 %reduce-scatter.13.cloned.1.call-start = ((), (), s32[]{:S(2)}) async-start(), calls=%async_computation.11 | async-start | bytes 1310720 | tf_op jit(solution)/shard_map/reduce_scatter | solution.py:37
  122.0 3.1 collective-permute-start
  150.0 60.7 %all-gather.7.cloned.1.call-start = ((), (), s32[]{:S(2)}) async-start(), calls=%async_computation.12 | async-start | bytes 1310720 | tf_op jit(solution)/shard_map/all_gather | solution.py:46
  183.9 55.1 %reduce-scatter.15.cloned.1.call-start = ((), (), s32[]{:S(2)}) async-start(), calls=%async_computation.13 | async-start | bytes 786432 | tf_op jit(solution)/shard_map/reduce_scatter | solution.py:50
  224.8 74.2 %reduce-scatter.17.cloned.1.call-start = ((), (), s32[]{:S(2)}) async-start(), calls=%async_computation.14 | async-start | bytes 1310720 | tf_op jit(solution)/shard_map/reduce_scatter | solution.py:37
  239.0 3.1 collective-permute-start.1
  266.9 60.6 %all-gather.9.cloned.1.call-start = ((), (), s32[]{:S(2)}) async-start(), calls=%async_computation.15 | async-start | bytes 1310720 | tf_op jit(solution)/shard_map/all_gather | solution.py:46
  300.9 55.1 %reduce-scatter.19.cloned.1.call-start = ((), (), s32[]{:S(2)}) async-start(), calls=%async_computation.16 | async-start | bytes 786432 | tf_op jit(solution)/shard_map/reduce_scatter | solution.py:50
  341.8 74.4 %reduce-scatter.21.cloned.1.call-start = ((), (), s32[]{:S(2)}) async-start(), calls=%async_computation.17 | async-start | bytes 1310720 | tf_op jit(solution)/shard_map/reduce_scatter | solution.py:37
  356.0 3.1 collective-permute-start.2
  384.1 60.6 %all-gather.11.cloned.1.call-start = ((), (), s32[]{:S(2)}) async-start(), calls=%async_computation.18 | async-start | bytes 1310720 | tf_op jit(solution)/shard_map/all_gather | solution.py:46
  418.0 55.2 %reduce-scatter.23.cloned.1.call-start = ((), (), s32[]{:S(2)}) async-start(), calls=%async_computation.19 | async-start | bytes 786432 | tf_op jit(solution)/shard_map/reduce_scatter | solution.py:50
  458.0 15.2 %copy-start = (bf16[1024,128]{0,1:T(8,128)(2,1)S(1)}, bf16[1024,128]{0,1:T(8,128)(2,1)}, u32[]{:S(2)}) copy-start(bf16[1024,128]{0,1:T(8,128)(2,1)} %reduce-scatter.11.cloned.1.call-done) | copy-start | bytes 786436
  458.0 15.2 %copy-start.1 = (bf16[1024,128]{0,1:T(8,128)(2,1)S(1)}, bf16[1024,128]{0,1:T(8,128)(2,1)}, u32[]{:S(2)}) copy-start(bf16[1024,128]{0,1:T(8,128)(2,1)} %reduce-scatter.15.cloned.1.call-done) | copy-start | bytes 786436
  458.0 15.2 %copy-start.2 = (bf16[1024,128]{0,1:T(8,128)(2,1)S(1)}, bf16[1024,128]{0,1:T(8,128)(2,1)}, u32[]{:S(2)}) copy-start(bf16[1024,128]{0,1:T(8,128)(2,1)} %reduce-scatter.19.cloned.1.call-done) | copy-start | bytes 786436
Sparse Core Ops, SparseCore 0:
  36.4 28.6 reduce-scatter.8
  67.0 26.5 all-gather.4
  107.9 14.0 reduce-scatter.10
  150.1 31.9 reduce-scatter.12
  184.0 26.5 all-gather.6
  224.9 14.0 reduce-scatter.14
  267.1 31.9 reduce-scatter.16
  301.0 26.5 all-gather.8
  341.9 14.0 reduce-scatter.18
  384.2 31.9 reduce-scatter.20
  418.1 26.5 all-gather.10
  459.1 14.0 reduce-scatter.22
where the time goes:
time: 483 us; the launch traced here: 482 us
  waiting for transfers between devices  291 us (60%)
  matrix products  118 us (24%)
  blocking collectives  31.3 us (6%)
  other arithmetic  17.6 us (4%)
  between operations  13.9 us (3%)
  starting transfers between devices  5.87 us (1%)
    reduce_scatter x4, waiting for transfers between devices, solve_section(): lax.psum_scatter(forward.astype(jnp.bfloat16), 'row', scatter_dimension=0...  124 us
    all_gather x4, waiting for transfers between devices, solve_section(): lax.all_gather(scaled, 'row', axis=0, tiled=True)  107 us
    dot_general x4, matrix products, solve_section(): jnp.einsum('kij,jb->kib', factor, lax.all_gather(source, 'col', axis=0, t...  65.2 us
    reduce_scatter x4, waiting for transfers between devices, solve_section(): lax.psum_scatter(back.astype(jnp.bfloat16), 'col', scatter_dimension=0, t...  56.6 us
    dot_general x4, matrix products, solve_section(): jnp.einsum('kij,ib->kjb', factor, lax.all_gather(scaled, 'row', axis=0, t...  52.8 us
    all_gather x4, blocking collectives, solve_section(): lax.all_gather(source, 'col', axis=0, tiled=True)  31.3 us
  transfers between devices with their start and end apart: 15, of which 15 were waited for; matrix products, arithmetic and copies ran while one was open for 0% of the time, Pallas kernels for 0%

commit v1 on v0

--- a/solution.py
+++ b/solution.py
@@ -2,6 +2,11 @@
 import jax.numpy as jnp
 from jax import lax
 from jax.sharding import PartitionSpec as P
+
+
+def tiled_gather(x, axis, dim):
+    copies = jnp.concatenate([x] * lax.axis_size(axis), axis=dim)
+    return lax.all_to_all(copies, axis, dim, dim, tiled=True)
 
 
 def shifted(value, axis, steps):
@@ -28,10 +33,7 @@
 def solve_section(source, factor, dinv):
     width = source.shape[1]
     product = jnp.einsum(
-        "kij,jb->kib",
-        factor,
-        lax.all_gather(source, "col", axis=0, tiled=True),
-        preferred_element_type=jnp.float32,
+        "kij,jb->kib", factor, tiled_gather(source, "col", 0), preferred_element_type=jnp.float32
     )
     forward = combine_stack(product)
     share = lax.psum_scatter(

time: 483 us -> 494 us (1.023)
  blocking collectives: 31.3 us -> 39 us
    all_to_all x0 -> x4, blocking collectives: none -> 39 us  [tiled_gather(): return lax.all_to_all(copies, axis, dim, dim, tiled=True)]
    all_gather x4 -> x0, blocking collectives: 31.3 us -> none  [solve_section(): lax.all_gather(source, 'col', axis=0, tiled=True)]
where the time goes in v1:
time: 494 us; the launch traced here: 493 us
  waiting for transfers between devices  290 us (59%)
  matrix products  118 us (24%)
  blocking collectives  39 us (8%)
  other arithmetic  17.8 us (4%)
  between operations  14 us (3%)
  local copies, waits for them, and re-layouts  7.78 us (2%)
  starting transfers between devices  5.91 us (1%)
    reduce_scatter x4, waiting for transfers between devices, solve_section(): lax.psum_scatter(forward.astype(jnp.bfloat16), 'row', scatter_dimension=0...  123 us
    all_gather x4, waiting for transfers between devices, solve_section(): lax.all_gather(scaled, 'row', axis=0, tiled=True)  107 us
    dot_general x4, matrix products, solve_section(): jnp.einsum('kij,jb->kib', factor, tiled_gather(source, 'col', 0), preferr...  65.3 us
    reduce_scatter x4, waiting for transfers between devices, solve_section(): lax.psum_scatter(back.astype(jnp.bfloat16), 'col', scatter_dimension=0, t...  56.6 us
    dot_general x4, matrix products, solve_section(): jnp.einsum('kij,ib->kjb', factor, lax.all_gather(scaled, 'row', axis=0, t...  52.8 us
    all_to_all x4, blocking collectives, tiled_gather(): return lax.all_to_all(copies, axis, dim, dim, tiled=True)  39 us
  transfers between devices with their start and end apart: 15, of which 15 were waited for; matrix products, arithmetic and copies ran while one was open for 0% of the time, Pallas kernels for 0%

profile of v1, /device:TPU:0, one launch (start us, length us, event | category | flops | bytes accessed | tf_op | source)
XLA Modules:
  0.0 493.0 jit_solution(3584544687681358770)
XLA Ops:
  6.5 0.8 fusion.80
  7.3 1.2 copy.7
  8.8 12.0 %all_to_all.48 = bf16[2,1024,128]{1,2,0:T(8,128)(2,1)S(1)} all-to-all(bf16[2,1024,128]{1,2,0:T(8,128)(2,1)S(1)} %bitcast.133), channel_id=1, replica_groups=mesh['sec'=4,'row'=4,'col'=2] {'col'}, dimensions={0} | all-to-all | bytes 1048576 | tf_op jit(solution)/shard_map/all_to_all | solution.py:9
  21.8 16.3 %fusion.16 = f32[2,4096,128]{1,2,0:T(8,128)S(1)} fusion(bf16[2048,128,1]{0,1,2:T(8,128)(2,1)S(1)} %reshape.97, bf16[1,2,4096,2048]{3,2,1,0:T(8,128)(2,1)} %param.5), kind=kOutput, calls=%fused_computation.16 | convolution fusion | flops 4294967296 | bytes 38273024 | tf_op jit(solution)/shard_map/kij,jb->kib/dot_general | solution.py:35
  38.3 1.1 pad_maximum_fusion
  39.4 0.9 constant_dynamic-slice_fusion
  40.3 26.8 %reduce-scatter.9.cloned.1.call-done = bf16[1024,128]{0,1:T(8,128)(2,1)} async-done(((bf16[4096,128]{0,1:T(8,128)(2,1)}), bf16[1024,128]{0,1:T(8,128)(2,1)}) %reduce-scatter.9.cloned.1.call-update) | async-done | bytes 262160 | tf_op jit(solution)/shard_map/reduce_scatter | solution.py:39
  67.1 1.0 convert_element_type.61
  68.2 0.7 pad_maximum_fusion.12
  69.0 26.7 %all-gather.5.cloned.1.call-done = bf16[4096,128]{0,1:T(8,128)(2,1)} async-done(((bf16[1024,128]{0,1:T(8,128)(2,1)}), bf16[4096,128]{0,1:T(8,128)(2,1)}) %all-gather.5.cloned.1.call-update) | async-done | bytes 1048592 | tf_op jit(solution)/shard_map/all_gather | solution.py:48
  95.7 13.2 %fusion.28 = f32[2,2048,128]{1,2,0:T(8,128)S(1)} fusion(bf16[1,2,4096,2048]{3,2,1,0:T(8,128)(2,1)} %param.5, bf16[4096,128]{0,1:T(8,128)(2,1)} %all-gather.5.cloned.1.call-done), kind=kOutput, calls=%fused_computation.20 | convolution fusion | flops 4294967296 | bytes 36700160 | tf_op jit(solution)/shard_map/kij,ib->kjb/dot_general | solution.py:45
  109.0 0.8 pad_maximum_fusion.5
  109.9 14.2 %reduce-scatter.11.cloned.1.call-done = bf16[1024,128]{0,1:T(8,128)(2,1)} async-done(((bf16[2048,128]{0,1:T(8,128)(2,1)}), bf16[1024,128]{0,1:T(8,128)(2,1)}) %reduce-scatter.11.cloned.1.call-update) | async-done | bytes 262160 | tf_op jit(solution)/shard_map/reduce_scatter | solution.py:52
  124.1 1.7 collective-permute-start
  125.8 1.3 collective-permute-done
  127.4 9.0 %all_to_all.49 = bf16[2,1024,128]{1,2,0:T(8,128)(2,1)S(1)} all-to-all(bf16[2,1024,128]{1,2,0:T(8,128)(2,1)S(1)} %bitcast.135), channel_id=1, replica_groups=mesh['sec'=4,'row'=4,'col'=2] {'col'}, dimensions={0} | all-to-all | bytes 1048576 | tf_op jit(solution)/shard_map/all_to_all | solution.py:9
  137.4 16.3 %fusion.19 = f32[2,4096,128]{1,2,0:T(8,128)S(1)} fusion(bf16[2048,128,1]{0,1,2:T(8,128)(2,1)S(1)} %reshape.99, bf16[1,2,4096,2048]{3,2,1,0:T(8,128)(2,1)} %param.5), kind=kOutput, calls=%fused_computation.17 | convolution fusion | flops 4294967296 | bytes 38273024 | tf_op jit(solution)/shard_map/kij,jb->kib/dot_general | solution.py:35
  153.9 1.1 pad_maximum_fusion.1
  155.0 32.0 %reduce-scatter.13.cloned.1.call-done = bf16[1024,128]{0,1:T(8,128)(2,1)} async-done(((bf16[4096,128]{0,1:T(8,128)(2,1)}), bf16[1024,128]{0,1:T(8,128)(2,1)}) %reduce-scatter.13.cloned.1.call-update) | async-done | bytes 262160 | tf_op jit(solution)/shard_map/reduce_scatter | solution.py:39
  187.1 1.0 convert_element_type.64
  189.0 26.7 %all-gather.7.cloned.1.call-done = bf16[4096,128]{0,1:T(8,128)(2,1)} async-done(((bf16[1024,128]{0,1:T(8,128)(2,1)}), bf16[4096,128]{0,1:T(8,128)(2,1)}) %all-gather.7.cloned.1.call-update) | async-done | bytes 1048592 | tf_op jit(solution)/shard_map/all_gather | solution.py:48
  215.7 13.2 %fusion.31 = f32[2,2048,128]{1,2,0:T(8,128)S(1)} fusion(bf16[1,2,4096,2048]{3,2,1,0:T(8,128)(2,1)} %param.5, bf16[4096,128]{0,1:T(8,128)(2,1)} %all-gather.7.cloned.1.call-done), kind=kOutput, calls=%fused_computation.21 | convolution fusion | flops 4294967296 | bytes 36700160 | tf_op jit(solution)/shard_map/kij,ib->kjb/dot_general | solution.py:45
  229.0 0.8 pad_maximum_fusion.7
  229.9 14.2 %reduce-scatter.15.cloned.1.call-done = bf16[1024,128]{0,1:T(8,128)(2,1)} async-done(((bf16[2048,128]{0,1:T(8,128)(2,1)}), bf16[1024,128]{0,1:T(8,128)(2,1)}) %reduce-scatter.15.cloned.1.call-update) | async-done | bytes 262160 | tf_op jit(solution)/shard_map/reduce_scatter | solution.py:52
  244.0 1.7 collective-permute-start.1
  245.8 1.3 collective-permute-done.1
  247.4 9.0 %all_to_all.50 = bf16[2,1024,128]{1,2,0:T(8,128)(2,1)S(1)} all-to-all(bf16[2,1024,128]{1,2,0:T(8,128)(2,1)S(1)} %bitcast.137), channel_id=1, replica_groups=mesh['sec'=4,'row'=4,'col'=2] {'col'}, dimensions={0} | all-to-all | bytes 1048576 | tf_op jit(solution)/shard_map/all_to_all | solution.py:9
  257.3 16.3 %fusion.22 = f32[2,4096,128]{1,2,0:T(8,128)S(1)} fusion(bf16[2048,128,1]{0,1,2:T(8,128)(2,1)S(1)} %reshape.101, bf16[1,2,4096,2048]{3,2,1,0:T(8,128)(2,1)} %param.5), kind=kOutput, calls=%fused_computation.18 | convolution fusion | flops 4294967296 | bytes 38273024 | tf_op jit(solution)/shard_map/kij,jb->kib/dot_general | solution.py:35
  273.9 1.1 pad_maximum_fusion.2
  275.0 32.0 %reduce-scatter.17.cloned.1.call-done = bf16[1024,128]{0,1:T(8,128)(2,1)} async-done(((bf16[4096,128]{0,1:T(8,128)(2,1)}), bf16[1024,128]{0,1:T(8,128)(2,1)}) %reduce-scatter.17.cloned.1.call-update) | async-done | bytes 262160 | tf_op jit(solution)/shard_map/reduce_scatter | solution.py:39
  307.0 1.0 convert_element_type.67
  309.1 26.5 %all-gather.9.cloned.1.call-done = bf16[4096,128]{0,1:T(8,128)(2,1)} async-done(((bf16[1024,128]{0,1:T(8,128)(2,1)}), bf16[4096,128]{0,1:T(8,128)(2,1)}) %all-gather.9.cloned.1.call-update) | async-done | bytes 1048592 | tf_op jit(solution)/shard_map/all_gather | solution.py:48
  335.6 13.2 %fusion.34 = f32[2,2048,128]{1,2,0:T(8,128)S(1)} fusion(bf16[1,2,4096,2048]{3,2,1,0:T(8,128)(2,1)} %param.5, bf16[4096,128]{0,1:T(8,128)(2,1)} %all-gather.9.cloned.1.call-done), kind=kOutput, calls=%fused_computation.22 | convolution fusion | flops 4294967296 | bytes 36700160 | tf_op jit(solution)/shard_map/kij,ib->kjb/dot_general | solution.py:45
  348.9 0.8 pad_maximum_fusion.9
  349.9 14.2 %reduce-scatter.19.cloned.1.call-done = bf16[1024,128]{0,1:T(8,128)(2,1)} async-done(((bf16[2048,128]{0,1:T(8,128)(2,1)}), bf16[1024,128]{0,1:T(8,128)(2,1)}) %reduce-scatter.19.cloned.1.call-update) | async-done | bytes 262160 | tf_op jit(solution)/shard_map/reduce_scatter | solution.py:52
  364.0 1.7 collective-permute-start.2
  365.8 1.3 collective-permute-done.2
  367.4 9.0 %all_to_all.51 = bf16[2,1024,128]{1,2,0:T(8,128)(2,1)S(1)} all-to-all(bf16[2,1024,128]{1,2,0:T(8,128)(2,1)S(1)} %bitcast.139), channel_id=1, replica_groups=mesh['sec'=4,'row'=4,'col'=2] {'col'}, dimensions={0} | all-to-all | bytes 1048576 | tf_op jit(solution)/shard_map/all_to_all | solution.py:9
  377.3 16.3 %fusion.25 = f32[2,4096,128]{1,2,0:T(8,128)S(1)} fusion(bf16[2048,128,1]{0,1,2:T(8,128)(2,1)S(1)} %reshape.103, bf16[1,2,4096,2048]{3,2,1,0:T(8,128)(2,1)} %param.5), kind=kOutput, calls=%fused_computation.19 | convolution fusion | flops 4294967296 | bytes 38273024 | tf_op jit(solution)/shard_map/kij,jb->kib/dot_general | solution.py:35
  393.9 1.1 pad_maximum_fusion.3
  395.0 32.0 %reduce-scatter.21.cloned.1.call-done = bf16[1024,128]{0,1:T(8,128)(2,1)} async-done(((bf16[4096,128]{0,1:T(8,128)(2,1)}), bf16[1024,128]{0,1:T(8,128)(2,1)}) %reduce-scatter.21.cloned.1.call-update) | async-done | bytes 262160 | tf_op jit(solution)/shard_map/reduce_scatter | solution.py:39
  427.0 1.0 convert_element_type.70
  428.9 26.7 %all-gather.11.cloned.1.call-done = bf16[4096,128]{0,1:T(8,128)(2,1)} async-done(((bf16[1024,128]{0,1:T(8,128)(2,1)}), bf16[4096,128]{0,1:T(8,128)(2,1)}) %all-gather.11.cloned.1.call-update) | async-done | bytes 1048592 | tf_op jit(solution)/shard_map/all_gather | solution.py:48
  455.6 13.2 %fusion.37 = f32[2,2048,128]{1,2,0:T(8,128)S(1)} fusion(bf16[1,2,4096,2048]{3,2,1,0:T(8,128)(2,1)} %param.5, bf16[4096,128]{0,1:T(8,128)(2,1)} %all-gather.11.cloned.1.call-done), kind=kOutput, calls=%fused_computation.23 | convolution fusion | flops 4294967296 | bytes 36700160 | tf_op jit(solution)/shard_map/kij,ib->kjb/dot_general | solution.py:45
  469.0 0.8 pad_maximum_fusion.11
  469.8 14.2 %reduce-scatter.23.cloned.1.call-done = bf16[1024,128]{0,1:T(8,128)(2,1)} async-done(((bf16[2048,128]{0,1:T(8,128)(2,1)}), bf16[1024,128]{0,1:T(8,128)(2,1)}) %reduce-scatter.23.cloned.1.call-update) | async-done | bytes 262160 | tf_op jit(solution)/shard_map/reduce_scatter | solution.py:52
  484.0 1.1 select_bitcast_fusion
  485.2 1.0 copy.16
  (74 shorter events, 9.3 us)
Async XLA Ops:
  6.5 60.6 %reduce-scatter.9.cloned.1.call-start = ((), (), s32[]{:S(2)}) async-start(), calls=%async_computation.12 | async-start | bytes 1310720 | tf_op jit(solution)/shard_map/reduce_scatter | solution.py:39
  39.4 56.3 %all-gather.5.cloned.1.call-start = ((), (), s32[]{:S(2)}) async-start(), calls=%async_computation.13 | async-start | bytes 1310720 | tf_op jit(solution)/shard_map/all_gather | solution.py:48
  68.9 55.1 %reduce-scatter.11.cloned.1.call-start = ((), (), s32[]{:S(2)}) async-start(), calls=%async_computation.14 | async-start | bytes 786432 | tf_op jit(solution)/shard_map/reduce_scatter | solution.py:52
  109.9 77.2 %reduce-scatter.13.cloned.1.call-start = ((), (), s32[]{:S(2)}) async-start(), calls=%async_computation.15 | async-start | bytes 1310720 | tf_op jit(solution)/shard_map/reduce_scatter | solution.py:39
  124.1 3.1 collective-permute-start
  155.0 60.7 %all-gather.7.cloned.1.call-start = ((), (), s32[]{:S(2)}) async-start(), calls=%async_computation.16 | async-start | bytes 1310720 | tf_op jit(solution)/shard_map/all_gather | solution.py:48
  188.9 55.1 %reduce-scatter.15.cloned.1.call-start = ((), (), s32[]{:S(2)}) async-start(), calls=%async_computation.17 | async-start | bytes 786432 | tf_op jit(solution)/shard_map/reduce_scatter | solution.py:52
  229.8 77.2 %reduce-scatter.17.cloned.1.call-start = ((), (), s32[]{:S(2)}) async-start(), calls=%async_computation.18 | async-start | bytes 1310720 | tf_op jit(solution)/shard_map/reduce_scatter | solution.py:39
  244.0 3.1 collective-permute-start.1
  275.0 60.7 %all-gather.9.cloned.1.call-start = ((), (), s32[]{:S(2)}) async-start(), calls=%async_computation.19 | async-start | bytes 1310720 | tf_op jit(solution)/shard_map/all_gather | solution.py:48
  308.9 55.1 %reduce-scatter.19.cloned.1.call-start = ((), (), s32[]{:S(2)}) async-start(), calls=%async_computation.20 | async-start | bytes 786432 | tf_op jit(solution)/shard_map/reduce_scatter | solution.py:52
  349.8 77.2 %reduce-scatter.21.cloned.1.call-start = ((), (), s32[]{:S(2)}) async-start(), calls=%async_computation.21 | async-start | bytes 1310720 | tf_op jit(solution)/shard_map/reduce_scatter | solution.py:39
  364.0 3.1 collective-permute-start.2
  394.9 60.7 %all-gather.11.cloned.1.call-start = ((), (), s32[]{:S(2)}) async-start(), calls=%async_computation.22 | async-start | bytes 1310720 | tf_op jit(solution)/shard_map/all_gather | solution.py:48
  428.8 55.2 %reduce-scatter.23.cloned.1.call-start = ((), (), s32[]{:S(2)}) async-start(), calls=%async_computation.23 | async-start | bytes 786432 | tf_op jit(solution)/shard_map/reduce_scatter | solution.py:52
  468.8 15.2 %copy-start = (bf16[1024,128]{0,1:T(8,128)(2,1)S(1)}, bf16[1024,128]{0,1:T(8,128)(2,1)}, u32[]{:S(2)}) copy-start(bf16[1024,128]{0,1:T(8,128)(2,1)} %reduce-scatter.11.cloned.1.call-done) | copy-start | bytes 786436
  468.8 15.2 %copy-start.1 = (bf16[1024,128]{0,1:T(8,128)(2,1)S(1)}, bf16[1024,128]{0,1:T(8,128)(2,1)}, u32[]{:S(2)}) copy-start(bf16[1024,128]{0,1:T(8,128)(2,1)} %reduce-scatter.15.cloned.1.call-done) | copy-start | bytes 786436
  468.8 15.2 %copy-start.2 = (bf16[1024,128]{0,1:T(8,128)(2,1)S(1)}, bf16[1024,128]{0,1:T(8,128)(2,1)}, u32[]{:S(2)}) copy-start(bf16[1024,128]{0,1:T(8,128)(2,1)} %reduce-scatter.19.cloned.1.call-done) | copy-start | bytes 786436
Sparse Core Ops, SparseCore 0:
  39.5 27.5 reduce-scatter.8
  69.1 26.5 all-gather.4
  110.0 14.0 reduce-scatter.10
  155.1 31.9 reduce-scatter.12
  189.0 26.5 all-gather.6
  229.9 14.0 reduce-scatter.14
  275.1 31.9 reduce-scatter.16
  309.0 26.5 all-gather.8
  349.9 14.0 reduce-scatter.18
  395.1 31.9 reduce-scatter.20
  429.0 26.5 all-gather.10
  469.9 14.0 reduce-scatter.22
